TPU v7x, 32 devices: a whole 2x2x4 slice. The times are simulated.
32 devices in a mesh: groups: 2 (over y), seq: 4 (over x, core), chan: 4 (over z).
Axes of the slice: x: 2, y: 2, z: 4, core: 2. Of those that a mesh axis runs over, the one named last changes fastest.
Arguments:
- tokens: bfloat16 [4096, 4096], P(('groups', 'seq'), 'chan'), parts along dimension 0, may hold values from -6 to 6
- norm_gain: float32 [4096], replicated, may hold values from 0.5 to 1.5
- proj_weight: bfloat16 [4096, 3, 4096], P('seq', None, 'chan'), may hold values from -0.09375 to 0.09375
- short_filter: float32 [3, 3, 4096], P(None, None, 'chan'), may hold values from -2.5 to 2.5
- long_filter: float32 [4096, 2048], P('chan', 'seq'), may hold values from -4 to 4, as said below
- skip_gain: float32 [4096], P('chan'), may hold values from 0.5 to 1.5
- out_weight: bfloat16 [4096, 4096], P(None, 'chan'), may hold values from -0.09375 to 0.09375
Outputs:
- block_out: bfloat16 [4096, 4096], P(('groups', 'seq'), 'chan'), parts along dimension 0
There are 2 independent parts, one for each index of `groups`. A program takes and returns all parts, laid end to end along the dimension named above; an argument that names none is the same for every part. Nothing has to cross between parts.
Inputs may be any that keep to these rules, and one draw needn't show every extreme that they name: `long_filter`: filter taps of the sequence-long convolution.
All inputs are finite; a program needn't handle non-finite values.
Results may differ from a plain program's by a relative error of at most 0.012.
Values may be sent and summed in bfloat16 or wider, within the bound.
A program may use at most 128 MiB of HBM per device.

v0:
```python
import math
import jax
import jax.numpy as jnp
from jax import lax
from jax.sharding import PartitionSpec as P

SHORT = 3
EPSILON = 1e-06
HIGHEST = lax.Precision.HIGHEST


def from_behind(value, axis, steps):
    count = lax.axis_size(axis)
    initial, last = (max(0, -steps), min(count, count - steps))
    return lax.ppermute(value, axis, [(source, source + steps) for source in range(initial, last)])


def angle_table(row_count, col_count, period, sign):
    row_index = lax.iota(jnp.int32, row_count)[:, None]
    col_index = lax.iota(jnp.int32, col_count)[None, :]
    angles = (row_index * col_index % period).astype(jnp.float32) * (sign * 2.0 * math.pi / period)
    return (jnp.cos(angles), jnp.sin(angles))


def forward_spectrum(signal_rows, first, second):
    channels = signal_rows.shape[0]
    grid_rows = signal_rows.reshape(channels, first, second)
    cos_first, sin_first = angle_table(first, first, first, -1.0)
    part_re = jnp.einsum("cab,ak->ckb", grid_rows, cos_first, precision=HIGHEST)
    part_im = jnp.einsum("cab,ak->ckb", grid_rows, sin_first, precision=HIGHEST)
    twist_cos, twist_sin = angle_table(first, second, first * second, -1.0)
    part_re, part_im = (
        part_re * twist_cos - part_im * twist_sin,
        part_re * twist_sin + part_im * twist_cos,
    )
    cos_second, sin_second = angle_table(second, second, second, -1.0)
    spectrum_real = jnp.einsum("ckb,bm->ckm", part_re, cos_second, precision=HIGHEST) - jnp.einsum(
        "ckb,bm->ckm", part_im, sin_second, precision=HIGHEST
    )
    spec_im = jnp.einsum("ckb,bm->ckm", part_re, sin_second, precision=HIGHEST) + jnp.einsum(
        "ckb,bm->ckm", part_im, cos_second, precision=HIGHEST
    )
    return (spectrum_real, spec_im)


def inverse_spectrum(spectrum_real, spec_im, first, second):
    channels = spectrum_real.shape[0]
    cos_second, sin_second = angle_table(second, second, second, 1.0)
    part_re = jnp.einsum("ckm,bm->ckb", spectrum_real, cos_second, precision=HIGHEST) - jnp.einsum(
        "ckm,bm->ckb", spec_im, sin_second, precision=HIGHEST
    )
    part_im = jnp.einsum("ckm,bm->ckb", spectrum_real, sin_second, precision=HIGHEST) + jnp.einsum(
        "ckm,bm->ckb", spec_im, cos_second, precision=HIGHEST
    )
    twist_cos, twist_sin = angle_table(first, second, first * second, 1.0)
    part_re, part_im = (
        part_re * twist_cos - part_im * twist_sin,
        part_re * twist_sin + part_im * twist_cos,
    )
    cos_first, sin_first = angle_table(first, first, first, 1.0)
    result = jnp.einsum("ckb,ak->cab", part_re, cos_first, precision=HIGHEST) - jnp.einsum(
        "ckb,ak->cab", part_im, sin_first, precision=HIGHEST
    )
    return result.reshape(channels, first * second) / (first * second)


def spectral_conv(signal_rows, filter_rows):
    channels, length = signal_rows.shape
    padded_len = 2 * length
    log_len = padded_len.bit_length() - 1
    first = 1 << log_len // 2
    second = padded_len // first
    zeros_tail = jnp.zeros((channels, length), jnp.float32)
    sig_re, sig_im = forward_spectrum(
        jnp.concatenate([signal_rows, zeros_tail], axis=1), first, second
    )
    tap_re, tap_im = forward_spectrum(
        jnp.concatenate([filter_rows, zeros_tail], axis=1), first, second
    )
    prod_re = sig_re * tap_re - sig_im * tap_im
    prod_im = sig_re * tap_im + sig_im * tap_re
    return inverse_spectrum(prod_re, prod_im, first, second)[:, :length]


def short_filter_output(projected, rim_cells, kernel_coefficients):
    count = kernel_coefficients.shape[0]
    steps_len = projected.shape[2]
    extended = jnp.concatenate([rim_cells, projected], axis=2).astype(jnp.float32)
    total = jnp.zeros(projected.shape, jnp.float32)
    for tap in range(count):
        total = (
            total
            + kernel_coefficients[tap][:, :, None]
            * extended[:, :, count - 1 - tap : count - 1 - tap + steps_len]
        )
    return total.astype(jnp.bfloat16)


def hyena_mixer(keys_rows, values_rows, long_taps, skip_part):
    middle = keys_rows.astype(jnp.float32) * values_rows.astype(jnp.float32)
    return (spectral_conv(middle, long_taps) + skip_part[:, None] * middle).astype(jnp.bfloat16)


def body(tokens, norm_gain, proj_weight, short_filter, long_filter, skip_gain, out_weight):
    seq_count = lax.axis_size("seq")
    local_rows = tokens.shape[0]
    local_chan = proj_weight.shape[2]
    subset = local_chan // seq_count
    length = local_rows * seq_count
    offset = lax.axis_index("seq") * subset
    whole = lax.all_gather(tokens, "chan", axis=1, tiled=True)
    wide = whole.astype(jnp.float32)
    rescaled_signal = (
        wide * lax.rsqrt(jnp.mean(wide * wide, axis=1, keepdims=True) + EPSILON) * norm_gain
    ).astype(jnp.bfloat16)
    projected = lax.dot_general(
        lax.all_gather(proj_weight, "seq", axis=0, tiled=True),
        rescaled_signal,
        (((0,), (1,)), ((), ())),
        preferred_element_type=jnp.float32,
    ).astype(jnp.bfloat16)
    taps_grid = long_filter.reshape(1, seq_count, subset, local_rows)
    long_taps = lax.all_to_all(taps_grid, "seq", split_axis=1, concat_axis=3, tiled=True).reshape(
        subset, length
    )
    skip_part = lax.dynamic_slice_in_dim(skip_gain, offset, subset, 0)
    rim_cells = from_behind(projected[:, :, local_rows - (SHORT - 1) :], "seq", 1)
    featured = short_filter_output(projected, rim_cells, short_filter)
    pair_grid = featured[1:].reshape(2, seq_count, subset, local_rows)
    moved = lax.all_to_all(pair_grid, "seq", split_axis=1, concat_axis=3, tiled=True).reshape(
        2, subset, length
    )
    result = hyena_mixer(moved[0], moved[1], long_taps, skip_part)
    returned = lax.all_to_all(
        result.reshape(1, subset, length), "seq", split_axis=2, concat_axis=0, tiled=True
    )
    returned = returned.reshape(local_chan, local_rows)
    gated = (featured[0].astype(jnp.float32) * returned.astype(jnp.float32)).astype(jnp.bfloat16)
    full_mix = lax.all_gather(gated, "chan", axis=0, tiled=True)
    update = lax.dot_general(
        full_mix, out_weight, (((0,), (0,)), ((), ())), preferred_element_type=jnp.float32
    )
    return (tokens.astype(jnp.float32) + update).astype(jnp.bfloat16)


def solution(mesh):
    placed = (
        P(("groups", "seq"), "chan"),
        P(),
        P("seq", None, "chan"),
        P(None, None, "chan"),
        P("chan", "seq"),
        P("chan"),
        P(None, "chan"),
    )
    return jax.shard_map(
        body, mesh=mesh, in_specs=placed, out_specs=P(("groups", "seq"), "chan"), check_vma=False
    )
```

profile of v0, /device:TPU:0, one launch (start us, length us, event | category | flops | bytes accessed | tf_op | source)
XLA Modules:
  0.0 568.1 jit_solution(13785095065940686060)
XLA Ops:
  12.3 80.1 %all-gather.4.cloned.1.call-done = bf16[512,4096]{1,0:T(8,128)(2,1)} async-done(((bf16[512,1024]{1,0:T(8,128)(2,1)}), bf16[512,4096]{1,0:T(8,128)(2,1)}) %all-gather.4.cloned.1.call-update) | async-done | bytes 4194320 | tf_op jit(solution)/shard_map/all_gather | solution.py:111
  95.5 151.8 %all-gather.6.cloned.1.call-done = bf16[4096,3,1024]{2,0,1:T(8,128)(2,1)} async-done(((bf16[1024,3,1024]{2,0,1:T(8,128)(2,1)}), bf16[4096,3,1024]{2,0,1:T(8,128)(2,1)}) %all-gather.6.cloned.1.call-update) | async-done | bytes 25165840 | tf_op jit(solution)/shard_map/all_gather | solution.py:117
  247.3 18.2 %convert_bitcast_fusion = bf16[3,1024,512]{1,2,0:T(8,128)(2,1)S(1)} fusion(bf16[4096,3,1024]{2,0,1:T(8,128)(2,1)} %all-gather.6.cloned.1.call-done, bf16[512,4096]{1,0:T(8,128)(2,1)} %all-gather.4.cloned.1.call-done, f32[4096]{0:T(1024)S(1)} %copy-done.5, f32[512]{0:T(512)S(1)} %add_rsqrt_fusion), kind=kOutput, calls=%fused_computation.53 | convolution fusion | flops 12894863360 | bytes 32524288 | tf_op jit(solution)/shard_map/dot_general | solution.py:116
  283.4 7.2 %fusion.23 = f32[64,256,64]{1,0,2:T(8,128)} fusion(f32[256,64,64]{0,2,1:T(8,128)S(1)} %bitcast.128), kind=kOutput, calls=%fused_computation.36 | convolution fusion | flops 805363712 | bytes 8388608 | tf_op jit(solution)/shard_map/cab,ak->ckb/dot_general | solution.py:30
  290.6 7.2 %fusion.25 = f32[64,256,64]{1,0,2:T(8,128)} fusion(f32[256,64,64]{0,2,1:T(8,128)S(1)} %bitcast.129), kind=kOutput, calls=%fused_computation.38 | convolution fusion | flops 805363712 | bytes 8388608 | tf_op jit(solution)/shard_map/cab,ak->ckb/dot_general | solution.py:29
  297.7 7.3 %all-to-all-done = bf16[2,4,256,512]{2,3,0,1:T(8,128)(2,1)} async-done(((bf16[2,4,256,512]{2,3,0,1:T(8,128)(2,1)}), bf16[2,4,256,512]{2,3,0,1:T(8,128)(2,1)}, u32[]{:S(2)}, u32[]{:S(2)}) %all-to-all-start) | async-done | bytes 2097184 | tf_op jit(solution)/shard_map/all_to_all | solution.py:130
  309.2 7.1 %fusion.35 = f32[64,256,64]{1,0,2:T(8,128)} fusion(f32[256,64,64]{0,2,1:T(8,128)S(1)} %bitcast.130), kind=kOutput, calls=%fused_computation.48 | convolution fusion | flops 805363712 | bytes 8388608 | tf_op jit(solution)/shard_map/cab,ak->ckb/dot_general | solution.py:30
  316.3 12.5 %subtract_bitcast_fusion = (f32[256,64,64]{0,1,2:T(8,128)S(1)}, f32[256,64,64]{0,1,2:T(8,128)S(1)}, f32[256,64,64]{0,1,2:T(8,128)S(1)}, f32[256,64,64]{0,1,2:T(8,128)S(1)}) fusion(f32[64,256,64]{1,0,2:T(8,128)} %fusion.23, f32[64,256,64]{1,0,2:T(8,128)} %fusion.25, f32[64,64]{0,1:T(8,128)S(1)} %copy.102, f32[64,64]{0,1:T(8,128)S(1)} %copy.99, ...), kind=kOutput, calls=%fused_computation.23 | convolution fusion | flops 817946624 | bytes 33587200 | tf_op jit(solution)/shard_map/cab,ak->ckb/dot_general | solution.py:29
  328.8 6.5 %fusion.15 = f32[256,64,64]{0,2,1:T(8,128)S(1)} fusion(f32[256,64,64]{0,1,2:T(8,128)S(1)} %get-tuple-element.10), kind=kOutput, calls=%fused_computation.28 | convolution fusion | flops 805363712 | bytes 8388608 | tf_op jit(solution)/shard_map/ckb,bm->ckm/dot_general | solution.py:40
  335.3 6.9 %fusion.17 = f32[256,64,64]{0,2,1:T(8,128)S(1)} fusion(f32[256,64,64]{0,1,2:T(8,128)S(1)} %get-tuple-element.10), kind=kOutput, calls=%fused_computation.30 | convolution fusion | flops 805363712 | bytes 8388608 | tf_op jit(solution)/shard_map/ckb,bm->ckm/dot_general | solution.py:37
  342.3 7.3 %fusion.27 = f32[256,64,64]{0,2,1:T(8,128)} fusion(f32[256,64,64]{0,1,2:T(8,128)S(1)} %get-tuple-element.13), kind=kOutput, calls=%fused_computation.40 | convolution fusion | flops 805363712 | bytes 8388608 | tf_op jit(solution)/shard_map/ckb,bm->ckm/dot_general | solution.py:40
  349.6 6.5 %fusion.29 = f32[256,64,64]{0,2,1:T(8,128)S(1)} fusion(f32[256,64,64]{0,1,2:T(8,128)S(1)} %get-tuple-element.13), kind=kOutput, calls=%fused_computation.42 | convolution fusion | flops 805363712 | bytes 8388608 | tf_op jit(solution)/shard_map/ckb,bm->ckm/dot_general | solution.py:37
  356.1 7.3 %fusion.47 = f32[256,64,64]{0,2,1:T(8,128)S(1)} fusion(f32[256,64,64]{0,2,1:T(8,128)S(1)} %fusion.17, f32[256,64,64]{0,1,2:T(8,128)S(1)} %get-tuple-element.9), kind=kOutput, calls=%fused_computation.56 | convolution fusion | flops 806412288 | bytes 12582912 | tf_op jit(solution)/shard_map/ckb,bm->ckm/dot_general | solution.py:37
  363.3 7.4 %fusion.50 = f32[256,64,64]{0,2,1:T(8,128)} fusion(f32[256,64,64]{0,2,1:T(8,128)S(1)} %fusion.15, f32[256,64,64]{0,1,2:T(8,128)S(1)} %get-tuple-element.9), kind=kOutput, calls=%fused_computation.57 | convolution fusion | flops 806412288 | bytes 12582912 | tf_op jit(solution)/shard_map/ckb,bm->ckm/dot_general | solution.py:40
  370.7 7.4 %fusion.41 = f32[256,64,64]{0,2,1:T(8,128)} fusion(f32[256,64,64]{0,2,1:T(8,128)S(1)} %fusion.29, f32[256,64,64]{0,1,2:T(8,128)S(1)} %get-tuple-element.14), kind=kOutput, calls=%fused_computation.54 | convolution fusion | flops 806412288 | bytes 12582912 | tf_op jit(solution)/shard_map/ckb,bm->ckm/dot_general | solution.py:37
  378.1 10.5 %multiply_add_fusion.1 = (f32[256,64,64]{0,2,1:T(8,128)S(1)}, f32[256,64,64]{0,2,1:T(8,128)S(1)}) fusion(f32[256,64,64]{0,2,1:T(8,128)S(1)} %fusion.47, f32[256,64,64]{0,2,1:T(8,128)} %fusion.41, f32[256,64,64]{0,2,1:T(8,128)} %fusion.50, f32[256,64,64]{0,2,1:T(8,128)} %fusion.27, f32[256,64,64]{0,1,2:T(8,128)S(1)} %get-tuple-element.14), kind=kOutput, calls=%fused_computation.20 | convolution fusion | flops 812703744 | bytes 29360128 | tf_op jit(solution)/shard_map/ckb,bm->ckm/dot_general | solution.py:40
  402.2 6.8 %multiply_subtract_fusion = (f32[256,64,64]{0,2,1:T(8,128)S(1)}, f32[256,64,64]{0,2,1:T(8,128)S(1)}) fusion(f32[256,64,64]{0,2,1:T(8,128)S(1)} %convolution_subtract_fusion, f32[64,64]{1,0:T(8,128)S(1)} %get-tuple-element.18, f32[64,64]{1,0:T(8,128)S(1)} %get-tuple-element.19, f32[256,64,64]{0,2,1:T(8,128)S(1)} %fusion.61, ...), kind=kOutput, calls=%fused_computation.19 | convolution fusion | flops 812703744 | bytes 21004288 | tf_op jit(solution)/shard_map/ckm,bm->ckb/dot_general | solution.py:52
  409.0 6.0 %fusion.9 = f32[64,256,64]{1,0,2:T(8,128)S(1)} fusion(f32[256,64,64]{0,2,1:T(8,128)S(1)} %get-tuple-element.8), kind=kOutput, calls=%fused_computation.13 | convolution fusion | flops 805363712 | bytes 8388608 | tf_op jit(solution)/shard_map/ckb,ak->cab/dot_general | solution.py:61
  415.1 6.4 %multiply_bitcast_fusion = f32[256,64,64]{0,1,2:T(8,128)S(1)} fusion(f32[64,256,64]{1,0,2:T(8,128)S(1)} %fusion.9, f32[256,64,64]{0,2,1:T(8,128)S(1)} %get-tuple-element.7), kind=kOutput, calls=%fused_computation.17 | convolution fusion | flops 807460864 | bytes 12582912 | tf_op jit(solution)/shard_map/ckb,ak->cab/dot_general | solution.py:61
  424.3 11.7 %copy.204 = bf16[1,256,2048]{1,0,2:T(2,128)(2,1)S(1)} copy(bf16[1,256,2048]{1,2,0:T(8,128)(2,1)S(1)} %fusion.57) | data formatting | bytes 2097152 | tf_op jit(solution)/shard_map/reshape | solution.py:135
  436.5 10.6 %reduce = bf16[2048,256]{1,0:T(8,128)(2,1)S(1)} reduce(bf16[2048,1,256]{2,1,0:T(2,128)(2,1)S(1)} %bitcast.137, bf16[]{:T(256)} %broadcast.298), dimensions={1}, to_apply=%bitcast.127.reduce_sub_computation | reduce | bytes 2097154
  447.5 17.1 %all_to_all.39 = bf16[4,2,65536]{2,1,0:T(2,128)(2,1)S(1)} all-to-all(bf16[4,2,65536]{2,1,0:T(2,128)(2,1)S(1)} %reshape.133), channel_id=1, replica_groups=mesh['groups'=2,'seq'=4,'chan'=4] {'seq'}, dimensions={0} | all-to-all | bytes 2097152 | tf_op jit(solution)/shard_map/all_to_all | solution.py:134
  470.3 80.9 %all-gather.8.cloned.1.call-done = bf16[4096,512]{0,1:T(8,128)(2,1)} async-done(((bf16[1024,512]{0,1:T(8,128)(2,1)}), bf16[4096,512]{0,1:T(8,128)(2,1)}) %all-gather.8.cloned.1.call-update) | async-done | bytes 4194320 | tf_op jit(solution)/shard_map/all_gather | solution.py:139
  551.2 10.1 %add_convert_fusion = bf16[512,1024]{1,0:T(8,128)(2,1)} fusion(bf16[512,1024]{1,0:T(8,128)(2,1)S(1)} %copy-done.3, bf16[4096,512]{0,1:T(8,128)(2,1)} %all-gather.8.cloned.1.call-done, bf16[4096,1024]{1,0:T(8,128)(2,1)} %param.13), kind=kOutput, calls=%fused_computation.67 | convolution fusion | flops 4296540160 | bytes 14680064 | tf_op jit(solution)/shard_map/dot_general | solution.py:140
  (55 shorter events, 53.7 us)
Async XLA Ops:
  6.5 85.9 %all-gather.4.cloned.1.call-start = ((), (), s32[]{:S(2)}) async-start(), calls=%async_computation.3 | async-start | bytes 5242880 | tf_op jit(solution)/shard_map/all_gather | solution.py:111
  7.3 240.0 %all-gather.6.cloned.1.call-start = ((), (), s32[]{:S(2)}) async-start(), calls=%async_computation.4 | async-start | bytes 31457280 | tf_op jit(solution)/shard_map/all_gather | solution.py:117
  8.0 239.3 %copy-start.5 = (f32[4096]{0:T(1024)S(1)}, f32[4096]{0:T(1024)}, u32[]{:S(2)}) copy-start(f32[4096]{0:T(1024)} %param.8) | copy-start | bytes 49156
  8.0 266.8 %all-to-all-start.1 = ((f32[1,4,256,512]{3,2,0,1:T(8,128)}), f32[1,4,256,512]{3,2,0,1:T(8,128)S(1)}, u32[]{:S(2)}, u32[]{:S(2)}) async-start(f32[1,4,256,512]{3,2,0,1:T(8,128)} %bitcast.143), calls=%async_computation.1 | async-start | bytes 4194304 | tf_op jit(solution)/shard_map/all_to_all | solution.py:123
  95.5 172.2 %copy-start.4 = (f32[3,3,1024]{2,1,0:T(4,128)S(1)}, f32[3,3,1024]{2,1,0:T(4,128)}, u32[]{:S(2)}) copy-start(f32[3,3,1024]{2,1,0:T(4,128)} %param.10) | copy-start | bytes 110596
  265.5 3.0 collective-permute-start
  271.5 1.6 copy-start.1
  274.8 6.2 %copy-start.2 = (f32[1,4,256,512]{3,2,0,1:T(8,128)}, f32[1,4,256,512]{3,2,0,1:T(8,128)S(1)}, u32[]{:S(2)}) copy-start(f32[1,4,256,512]{3,2,0,1:T(8,128)S(1)} %all-to-all-done.1) | copy-start | bytes 6291460
  274.9 30.2 %all-to-all-start = ((bf16[2,4,256,512]{2,3,0,1:T(8,128)(2,1)}), bf16[2,4,256,512]{2,3,0,1:T(8,128)(2,1)}, u32[]{:S(2)}, u32[]{:S(2)}) async-start(bf16[2,4,256,512]{2,3,0,1:T(8,128)(2,1)} %bitcast.136), calls=%async_computation | async-start | bytes 4194304 | tf_op jit(solution)/shard_map/all_to_all | solution.py:130
  279.3 271.9 %all-gather.8.cloned.1.call-start = ((), (), s32[]{:S(2)}) async-start(), calls=%async_computation.5 | async-start | bytes 5242880 | tf_op jit(solution)/shard_map/all_gather | solution.py:139
  307.3 1.9 copy-start
  467.2 84.0 %copy-start.3 = (bf16[512,1024]{1,0:T(8,128)(2,1)S(1)}, bf16[512,1024]{1,0:T(8,128)(2,1)}, u32[]{:S(2)}) copy-start(bf16[512,1024]{1,0:T(8,128)(2,1)} %param.7) | copy-start | bytes 3145732
Sparse Core Ops, SparseCore 0:
  8.9 83.4 all-gather.3
  94.0 153.2 all-gather.5
  470.5 80.7 all-gather.7
where the time goes:
time: 574 us; the launch traced here: 568 us
  waiting for transfers between devices  322 us (56%)
  matrix products  155 us (27%)
  local copies, waits for them, and re-layouts  28.4 us (5%)
  other arithmetic  20.5 us (4%)
  blocking collectives  17.1 us (3%)
  between operations  13.7 us (2%)
  starting transfers between devices  11.4 us (2%)
    all_gather x1, waiting for transfers between devices, body(): lax.all_gather(proj_weight, 'seq', axis=0, tiled=True)  152 us
    all_gather x1, waiting for transfers between devices, body(): full_mix = lax.all_gather(gated, 'chan', axis=0, tiled=True)  80.9 us
    all_gather x1, waiting for transfers between devices, body(): whole = lax.all_gather(tokens, 'chan', axis=1, tiled=True)  80.1 us
    dot_general x2, matrix products, forward_spectrum(): part_re = jnp.einsum('cab,ak->ckb', grid_rows, cos_first, precision=HIGHEST)  19.7 us
    dot_general x1, matrix products, body(): lax.dot_general(lax.all_gather(proj_weight, 'seq', axis=0, tiled=True), r...  18.2 us
    dot_general x2, matrix products, forward_spectrum(): jnp.einsum('ckb,bm->ckm', part_re, sin_second, precision=HIGHEST)  17.9 us
    all_to_all x1, blocking collectives, body(): lax.all_to_all(result.reshape(1, subset, length), 'seq', split_axis=2, co...  17.1 us
    dot_general x2, matrix products, forward_spectrum(): jnp.einsum('ckb,bm->ckm', part_re, cos_second, precision=HIGHEST)  14.6 us
  transfers between devices with their start and end apart: 6, of which 5 were waited for; matrix products, arithmetic and copies ran while one was open for 8% of the time, Pallas kernels for 0%

commit v1 on v0

--- a/solution.py
+++ b/solution.py
@@ -108,7 +108,7 @@
     subset = local_chan // seq_count
     length = local_rows * seq_count
     offset = lax.axis_index("seq") * subset
-    whole = lax.all_gather(tokens, "chan", axis=1, tiled=True)
+    whole = jnp.concatenate(lax.all_gather(tokens, "chan"), axis=1)
     wide = whole.astype(jnp.float32)
     rescaled_signal = (
         wide * lax.rsqrt(jnp.mean(wide * wide, axis=1, keepdims=True) + EPSILON) * norm_gain

time: 574 us -> 576 us (level)
  waiting for transfers between devices: 322 us -> 316 us
    all_gather x1, waiting for transfers between devices: 152 us -> 145 us  [body(): lax.all_gather(proj_weight, 'seq', axis=0, tiled=True)]
    unnamed x1 -> x2, other arithmetic: 10.6 us -> 13.8 us
  transfers between devices with their start and end apart: 6 -> 6, of which waited for: 5 -> 5; matrix products, arithmetic and copies ran while one was open for 8% -> 9% of each run, Pallas kernels for 0% -> 0%
where the time goes in v1:
time: 576 us; the launch traced here: 570 us
  waiting for transfers between devices  316 us (55%)
  matrix products  156 us (27%)
  local copies, waits for them, and re-layouts  34 us (6%)
  other arithmetic  21.5 us (4%)
  blocking collectives  17.1 us (3%)
  between operations  13.9 us (2%)
  starting transfers between devices  11.4 us (2%)
    all_gather x1, waiting for transfers between devices, body(): lax.all_gather(proj_weight, 'seq', axis=0, tiled=True)  145 us
    all_gather x1, waiting for transfers between devices, body(): full_mix = lax.all_gather(gated, 'chan', axis=0, tiled=True)  80.9 us
    all_gather x1, waiting for transfers between devices, body(): whole = jnp.concatenate(lax.all_gather(tokens, 'chan'), axis=1)  80.1 us
    dot_general x2, matrix products, forward_spectrum(): part_re = jnp.einsum('cab,ak->ckb', grid_rows, cos_first, precision=HIGHEST)  19.7 us
    dot_general x1, matrix products, body(): lax.dot_general(lax.all_gather(proj_weight, 'seq', axis=0, tiled=True), r...  19.4 us
    dot_general x2, matrix products, forward_spectrum(): jnp.einsum('ckb,bm->ckm', part_re, sin_second, precision=HIGHEST)  17.8 us
    all_to_all x1, blocking collectives, body(): lax.all_to_all(result.reshape(1, subset, length), 'seq', split_axis=2, co...  17.1 us
    dot_general x2, matrix products, forward_spectrum(): jnp.einsum('ckb,bm->ckm', part_re, cos_second, precision=HIGHEST)  14.8 us
  transfers between devices with their start and end apart: 6, of which 5 were waited for; matrix products, arithmetic and copies ran while one was open for 9% of the time, Pallas kernels for 0%

profile of v1, /device:TPU:0, one launch (start us, length us, event | category | flops | bytes accessed | tf_op | source)
XLA Modules:
  0.0 569.6 jit_solution(14978163512061516414)
XLA Ops:
  12.3 80.1 %all-gather.9.cloned.1.call-done = bf16[2048,1024]{1,0:T(8,128)(2,1)} async-done(((bf16[512,1024]{1,0:T(8,128)(2,1)}), bf16[2048,1024]{1,0:T(8,128)(2,1)}) %all-gather.9.cloned.1.call-update) | async-done | bytes 4194320 | tf_op jit(solution)/shard_map/all_gather | solution.py:111
  102.1 145.2 %all-gather.5.cloned.1.call-done = bf16[4096,3,1024]{2,0,1:T(8,128)(2,1)} async-done(((bf16[1024,3,1024]{2,0,1:T(8,128)(2,1)}), bf16[4096,3,1024]{2,0,1:T(8,128)(2,1)}) %all-gather.5.cloned.1.call-update) | async-done | bytes 25165840 | tf_op jit(solution)/shard_map/all_gather | solution.py:117
  247.3 19.4 %convert_bitcast_fusion.1 = bf16[3,1024,512]{1,2,0:T(8,128)(2,1)S(1)} fusion(bf16[4096,3,1024]{2,0,1:T(8,128)(2,1)} %all-gather.5.cloned.1.call-done, f32[512,4096]{1,0:T(8,128)} %bitcast.144, f32[4096]{0:T(1024)S(1)} %copy-done.6, f32[512]{0:T(512)S(1)} %add_rsqrt_fusion), kind=kOutput, calls=%fused_computation.52 | convolution fusion | flops 12892766208 | bytes 36718592 | tf_op jit(solution)/shard_map/dot_general | solution.py:116
  284.6 7.2 %fusion.21 = f32[64,256,64]{1,0,2:T(8,128)} fusion(f32[256,64,64]{0,2,1:T(8,128)S(1)} %bitcast.135), kind=kOutput, calls=%fused_computation.35 | convolution fusion | flops 805363712 | bytes 8388608 | tf_op jit(solution)/shard_map/cab,ak->ckb/dot_general | solution.py:30
  291.8 7.2 %fusion.23 = f32[64,256,64]{1,0,2:T(8,128)} fusion(f32[256,64,64]{0,2,1:T(8,128)S(1)} %bitcast.136), kind=kOutput, calls=%fused_computation.37 | convolution fusion | flops 805363712 | bytes 8388608 | tf_op jit(solution)/shard_map/cab,ak->ckb/dot_general | solution.py:29
  298.9 7.3 %all-to-all-done = bf16[2,4,256,512]{2,3,0,1:T(8,128)(2,1)} async-done(((bf16[2,4,256,512]{2,3,0,1:T(8,128)(2,1)}), bf16[2,4,256,512]{2,3,0,1:T(8,128)(2,1)}, u32[]{:S(2)}, u32[]{:S(2)}) %all-to-all-start) | async-done | bytes 2097184 | tf_op jit(solution)/shard_map/all_to_all | solution.py:130
  310.4 7.1 %fusion.33 = f32[64,256,64]{1,0,2:T(8,128)} fusion(f32[256,64,64]{0,2,1:T(8,128)S(1)} %bitcast.137), kind=kOutput, calls=%fused_computation.47 | convolution fusion | flops 805363712 | bytes 8388608 | tf_op jit(solution)/shard_map/cab,ak->ckb/dot_general | solution.py:30
  317.5 12.5 %subtract_bitcast_fusion = (f32[256,64,64]{0,1,2:T(8,128)S(1)}, f32[256,64,64]{0,1,2:T(8,128)S(1)}, f32[256,64,64]{0,1,2:T(8,128)S(1)}, f32[256,64,64]{0,1,2:T(8,128)S(1)}) fusion(f32[64,256,64]{1,0,2:T(8,128)} %fusion.21, f32[64,256,64]{1,0,2:T(8,128)} %fusion.23, f32[64,64]{0,1:T(8,128)S(1)} %copy.106, f32[64,64]{0,1:T(8,128)S(1)} %copy.103, ...), kind=kOutput, calls=%fused_computation.22 | convolution fusion | flops 817946624 | bytes 33587200 | tf_op jit(solution)/shard_map/cab,ak->ckb/dot_general | solution.py:29
  330.0 6.5 %fusion.13 = f32[256,64,64]{0,2,1:T(8,128)S(1)} fusion(f32[256,64,64]{0,1,2:T(8,128)S(1)} %get-tuple-element.10), kind=kOutput, calls=%fused_computation.27 | convolution fusion | flops 805363712 | bytes 8388608 | tf_op jit(solution)/shard_map/ckb,bm->ckm/dot_general | solution.py:40
  336.6 6.9 %fusion.15 = f32[256,64,64]{0,2,1:T(8,128)S(1)} fusion(f32[256,64,64]{0,1,2:T(8,128)S(1)} %get-tuple-element.10), kind=kOutput, calls=%fused_computation.29 | convolution fusion | flops 805363712 | bytes 8388608 | tf_op jit(solution)/shard_map/ckb,bm->ckm/dot_general | solution.py:37
  343.5 6.5 %fusion.27 = f32[256,64,64]{0,2,1:T(8,128)S(1)} fusion(f32[256,64,64]{0,1,2:T(8,128)S(1)} %get-tuple-element.13), kind=kOutput, calls=%fused_computation.41 | convolution fusion | flops 805363712 | bytes 8388608 | tf_op jit(solution)/shard_map/ckb,bm->ckm/dot_general | solution.py:37
  350.0 7.4 %fusion.25 = f32[256,64,64]{0,2,1:T(8,128)} fusion(f32[256,64,64]{0,1,2:T(8,128)S(1)} %get-tuple-element.13), kind=kOutput, calls=%fused_computation.39 | convolution fusion | flops 805363712 | bytes 8388608 | tf_op jit(solution)/shard_map/ckb,bm->ckm/dot_general | solution.py:40
  357.4 7.1 %fusion.48 = f32[256,64,64]{0,2,1:T(8,128)S(1)} fusion(f32[256,64,64]{0,2,1:T(8,128)S(1)} %fusion.13, f32[256,64,64]{0,1,2:T(8,128)S(1)} %get-tuple-element.9), kind=kOutput, calls=%fused_computation.56 | convolution fusion | flops 806412288 | bytes 12582912 | tf_op jit(solution)/shard_map/ckb,bm->ckm/dot_general | solution.py:40
  364.5 7.4 %fusion.45 = f32[256,64,64]{0,2,1:T(8,128)} fusion(f32[256,64,64]{0,2,1:T(8,128)S(1)} %fusion.15, f32[256,64,64]{0,1,2:T(8,128)S(1)} %get-tuple-element.9), kind=kOutput, calls=%fused_computation.55 | convolution fusion | flops 806412288 | bytes 12582912 | tf_op jit(solution)/shard_map/ckb,bm->ckm/dot_general | solution.py:37
  371.9 7.4 %fusion.39 = f32[256,64,64]{0,2,1:T(8,128)} fusion(f32[256,64,64]{0,2,1:T(8,128)S(1)} %fusion.27, f32[256,64,64]{0,1,2:T(8,128)S(1)} %get-tuple-element.14), kind=kOutput, calls=%fused_computation.53 | convolution fusion | flops 806412288 | bytes 12582912 | tf_op jit(solution)/shard_map/ckb,bm->ckm/dot_general | solution.py:37
  379.3 10.7 %multiply_add_fusion.1 = (f32[256,64,64]{0,2,1:T(8,128)S(1)}, f32[256,64,64]{0,2,1:T(8,128)S(1)}) fusion(f32[256,64,64]{0,2,1:T(8,128)} %fusion.45, f32[256,64,64]{0,2,1:T(8,128)} %fusion.39, f32[256,64,64]{0,2,1:T(8,128)S(1)} %fusion.48, f32[256,64,64]{0,2,1:T(8,128)} %fusion.25, f32[256,64,64]{0,1,2:T(8,128)S(1)} %get-tuple-element.14), kind=kOutput, calls=%fused_computation.19 | convolution fusion | flops 812703744 | bytes 29360128 | tf_op jit(solution)/shard_map/ckb,bm->ckm/dot_general | solution.py:40
  403.4 6.8 %multiply_subtract_fusion = (f32[256,64,64]{0,2,1:T(8,128)S(1)}, f32[256,64,64]{0,2,1:T(8,128)S(1)}) fusion(f32[256,64,64]{0,2,1:T(8,128)S(1)} %convolution_subtract_fusion, f32[64,64]{1,0:T(8,128)S(1)} %get-tuple-element.18, f32[64,64]{1,0:T(8,128)S(1)} %get-tuple-element.19, f32[256,64,64]{0,2,1:T(8,128)S(1)} %fusion.59, ...), kind=kOutput, calls=%fused_computation.18 | convolution fusion | flops 812703744 | bytes 21004288 | tf_op jit(solution)/shard_map/ckm,bm->ckb/dot_general | solution.py:52
  410.2 6.0 %fusion.7 = f32[64,256,64]{1,0,2:T(8,128)S(1)} fusion(f32[256,64,64]{0,2,1:T(8,128)S(1)} %get-tuple-element.8), kind=kOutput, calls=%fused_computation.12 | convolution fusion | flops 805363712 | bytes 8388608 | tf_op jit(solution)/shard_map/ckb,ak->cab/dot_general | solution.py:61
  416.2 6.4 %multiply_bitcast_fusion = f32[256,64,64]{0,1,2:T(8,128)S(1)} fusion(f32[64,256,64]{1,0,2:T(8,128)S(1)} %fusion.7, f32[256,64,64]{0,2,1:T(8,128)S(1)} %get-tuple-element.7), kind=kOutput, calls=%fused_computation.16 | convolution fusion | flops 807460864 | bytes 12582912 | tf_op jit(solution)/shard_map/ckb,ak->cab/dot_general | solution.py:61
  425.5 11.7 %copy.209 = bf16[1,256,2048]{1,0,2:T(2,128)(2,1)S(1)} copy(bf16[1,256,2048]{1,2,0:T(8,128)(2,1)S(1)} %fusion.55) | data formatting | bytes 2097152 | tf_op jit(solution)/shard_map/reshape | solution.py:135
  437.7 10.6 %reduce.2 = bf16[2048,256]{1,0:T(8,128)(2,1)S(1)} reduce(bf16[2048,1,256]{2,1,0:T(2,128)(2,1)S(1)} %bitcast.146, bf16[]{:T(256)} %broadcast.298), dimensions={1}, to_apply=%bitcast.134.reduce_sub_computation | reduce | bytes 2097154
  448.7 17.1 %all_to_all.39 = bf16[4,2,65536]{2,1,0:T(2,128)(2,1)S(1)} all-to-all(bf16[4,2,65536]{2,1,0:T(2,128)(2,1)S(1)} %reshape.141), channel_id=1, replica_groups=mesh['groups'=2,'seq'=4,'chan'=4] {'seq'}, dimensions={0} | all-to-all | bytes 2097152 | tf_op jit(solution)/shard_map/all_to_all | solution.py:134
  471.6 80.9 %all-gather.7.cloned.1.call-done = bf16[4096,512]{0,1:T(8,128)(2,1)} async-done(((bf16[1024,512]{0,1:T(8,128)(2,1)}), bf16[4096,512]{0,1:T(8,128)(2,1)}) %all-gather.7.cloned.1.call-update) | async-done | bytes 4194320 | tf_op jit(solution)/shard_map/all_gather | solution.py:139
  552.5 10.1 %add_convert_fusion = bf16[512,1024]{1,0:T(8,128)(2,1)} fusion(bf16[512,1024]{1,0:T(8,128)(2,1)S(1)} %copy-done.4, bf16[4096,512]{0,1:T(8,128)(2,1)} %all-gather.7.cloned.1.call-done, bf16[4096,1024]{1,0:T(8,128)(2,1)} %param.13), kind=kOutput, calls=%fused_computation.66 | convolution fusion | flops 4296540160 | bytes 14680064 | tf_op jit(solution)/shard_map/dot_general | solution.py:140
  (59 shorter events, 60.1 us)
Async XLA Ops:
  6.5 85.9 %all-gather.9.cloned.1.call-start = ((), (), s32[]{:S(2)}) async-start(), calls=%async_computation.5 | async-start | bytes 5242880 | tf_op jit(solution)/shard_map/all_gather | solution.py:111
  7.3 240.0 %all-gather.5.cloned.1.call-start = ((), (), s32[]{:S(2)}) async-start(), calls=%async_computation.3 | async-start | bytes 31457280 | tf_op jit(solution)/shard_map/all_gather | solution.py:117
  8.0 268.0 %all-to-all-start.1 = ((f32[1,4,256,512]{3,2,0,1:T(8,128)}), f32[1,4,256,512]{3,2,0,1:T(8,128)S(1)}, u32[]{:S(2)}, u32[]{:S(2)}) async-start(f32[1,4,256,512]{3,2,0,1:T(8,128)} %bitcast.152), calls=%async_computation.1 | async-start | bytes 4194304 | tf_op jit(solution)/shard_map/all_to_all | solution.py:123
  95.6 5.6 copy-start.1
  101.2 146.1 %copy-start.6 = (f32[4096]{0:T(1024)S(1)}, f32[4096]{0:T(1024)}, u32[]{:S(2)}) copy-start(f32[4096]{0:T(1024)} %param.8) | copy-start | bytes 49156
  247.3 21.6 %copy-start.5 = (f32[3,3,1024]{2,1,0:T(4,128)S(1)}, f32[3,3,1024]{2,1,0:T(4,128)}, u32[]{:S(2)}) copy-start(f32[3,3,1024]{2,1,0:T(4,128)} %param.10) | copy-start | bytes 110596
  266.7 3.0 collective-permute-start
  272.7 1.7 copy-start.2
  276.0 6.2 %copy-start.3 = (f32[1,4,256,512]{3,2,0,1:T(8,128)}, f32[1,4,256,512]{3,2,0,1:T(8,128)S(1)}, u32[]{:S(2)}) copy-start(f32[1,4,256,512]{3,2,0,1:T(8,128)S(1)} %all-to-all-done.1) | copy-start | bytes 6291460
  276.0 30.2 %all-to-all-start = ((bf16[2,4,256,512]{2,3,0,1:T(8,128)(2,1)}), bf16[2,4,256,512]{2,3,0,1:T(8,128)(2,1)}, u32[]{:S(2)}, u32[]{:S(2)}) async-start(bf16[2,4,256,512]{2,3,0,1:T(8,128)(2,1)} %bitcast.145), calls=%async_computation | async-start | bytes 4194304 | tf_op jit(solution)/shard_map/all_to_all | solution.py:130
  280.5 272.0 %all-gather.7.cloned.1.call-start = ((), (), s32[]{:S(2)}) async-start(), calls=%async_computation.4 | async-start | bytes 5242880 | tf_op jit(solution)/shard_map/all_gather | solution.py:139
  308.5 1.9 copy-start
  468.5 84.0 %copy-start.4 = (bf16[512,1024]{1,0:T(8,128)(2,1)S(1)}, bf16[512,1024]{1,0:T(8,128)(2,1)}, u32[]{:S(2)}) copy-start(bf16[512,1024]{1,0:T(8,128)(2,1)} %param.7) | copy-start | bytes 3145732
Sparse Core Ops, SparseCore 0:
  8.9 83.4 all-gather.8
  94.0 153.2 all-gather.4
  471.7 80.7 all-gather.6
